TPU v7x, 256 devices: a whole 4x4x8 slice. The times are simulated.
256 devices in a mesh: req: 32 (over z, x), tp: 8 (over y, core).
Axes of the slice: x: 4, y: 4, z: 8, core: 2. Of those that a mesh axis runs over, the one named last changes fastest.
Arguments:
- hidden_in: bfloat16 [32768, 2048], P('req'), may hold values from -6 to 6
- qkv_weight: bfloat16 [2048, 3, 2048], P(None, None, 'tp'), may hold values from -0.125 to 0.125
- out_weight: bfloat16 [2048, 2048], P('tp'), may hold values from -1.5 to 1.5
- kv_pool: bfloat16 [512, 2, 128, 2048], P('req', None, None, 'tp'), may hold values from -48 to 48
- cached_len: int32 [32], replicated, may hold values from 3585 to 4096, as said below
- page_slot: int32 [32, 32], replicated, may hold values from 0 to 15
- page_holder: int32 [32, 32, 1], replicated, may hold values from 0 to 31; in each aligned block of 32 rows (0 to 31, 32 to 63, ..., all dimensions but the last counted through in order) at most 2 rows name the same one
- cont_flag: int32 [32], replicated, may hold values 0 or 1
Outputs:
- attn_out: bfloat16 [32768, 2048], P(('req', 'tp'))
Inputs may be any that keep to these rules, and one draw needn't show every extreme that they name: `page_holder`: within the table entries of the requests of one index of req (aligned blocks of 1 request), no holder is named more than 2 times. `cached_len`: A cached length of 4096 occurs in every draw. `page_slot`: page slot k of holder h is row h * 16 + k of kv_pool.
All inputs are finite; a program needn't handle non-finite values.
Results may differ from a plain program's by a relative error of at most 0.02.
Values may be sent and summed in bfloat16 or wider, within the bound.
A program may use at most 128 MiB of HBM per device.

v0:
```python
import jax
import jax.numpy as jnp
from jax import lax
from jax.sharding import PartitionSpec as P

HD = 128
NEW = 1024
PAGE = 128
MAXP = 32


def rotate(feature, position):
    half_width = feature.shape[-1] // 2
    indices = jnp.arange(half_width).astype(jnp.float32)
    inverse = jnp.exp(indices * (-2.0 / feature.shape[-1]) * jnp.log(jnp.float32(10000.0)))
    angles = position[:, None, None] * inverse[None, None, :]
    cosine = jnp.cos(angles)
    sine_part = jnp.sin(angles)
    first_half = feature[..., :half_width]
    second_half = feature[..., half_width:]
    return jnp.concatenate(
        [
            first_half * cosine - second_half * sine_part,
            second_half * cosine + first_half * sine_part,
        ],
        axis=-1,
    )


def attend_block(query_part, keys_part, values_part, allowed):
    scores = jnp.einsum(
        "qd,kd->qk", query_part, keys_part, preferred_element_type=jnp.float32
    ) * HD ** (-0.5)
    scores = jnp.where(allowed, scores, -1e30)
    row_top = jnp.max(scores, axis=-1)
    weights = jnp.where(allowed, jnp.exp(scores - row_top[:, None]), 0.0)
    row_total = jnp.sum(weights, axis=-1)
    summed = jnp.einsum(
        "qk,kd->qd", weights.astype(jnp.bfloat16), values_part, preferred_element_type=jnp.float32
    )
    return (summed, row_top, row_total)


def body(hidden_in, qkv_weight, out_weight, kv_pool, cached_len, page_slot, page_holder, cont_flag):
    req_count = lax.axis_size("req")
    tp_count = lax.axis_size("tp")
    req_index = lax.axis_index("req")
    local_reqs = hidden_in.shape[0] // NEW
    local_width = qkv_weight.shape[2]
    local_heads = local_width // HD
    cache_span = MAXP * PAGE
    holder_rows = page_holder[:, :, 0]
    all_rows = holder_rows.shape[0]
    same_holder_all = holder_rows[:, :, None] == holder_rows[:, None, :]
    entry_ids = jnp.arange(holder_rows.shape[1])
    earlier_all = entry_ids[None, None, :] < entry_ids[None, :, None]
    rank_all = jnp.sum((same_holder_all & earlier_all).astype(jnp.int32), axis=2)
    first_hit = (holder_rows == req_index) & (rank_all == 0)
    send_slots = jnp.sum(jnp.where(first_hit, page_slot, 0), axis=1)
    outgoing = kv_pool[send_slots]
    spill_flat = (rank_all > 0).reshape(-1)
    spill_pos = jnp.cumsum(spill_flat.astype(jnp.int32)) - 1
    spill_count = jnp.sum(spill_flat.astype(jnp.int32))
    holders_flat = holder_rows.reshape(-1)
    slots_flat = page_slot.reshape(-1)
    lengths = lax.dynamic_slice_in_dim(cached_len, req_index * local_reqs, local_reqs)
    flags = lax.dynamic_slice_in_dim(cont_flag, req_index * local_reqs, local_reqs)
    live_len = lengths * flags
    token_rows = hidden_in.astype(jnp.float32)
    centre = jnp.mean(token_rows, axis=-1, keepdims=True)
    centred = token_rows - centre
    spread = jnp.mean(centred * centred, axis=-1, keepdims=True)
    normed = (centred * lax.rsqrt(spread + 1e-05)).astype(jnp.bfloat16)
    united_qkv = jnp.einsum("td,dcf->tcf", normed, qkv_weight, preferred_element_type=jnp.float32)
    positions = (live_len[:, None] + jnp.arange(NEW)[None, :]).astype(jnp.float32).reshape(-1)
    query_rot = rotate(united_qkv[:, 0].reshape(-1, local_heads, HD), positions).astype(
        jnp.bfloat16
    )
    new_key = rotate(united_qkv[:, 1].reshape(-1, local_heads, HD), positions).astype(jnp.bfloat16)
    new_value = united_qkv[:, 2].reshape(-1, local_heads, HD).astype(jnp.bfloat16)
    row_count = local_reqs * NEW
    block_rows = min(512, NEW)
    req_blocks = NEW // block_rows
    row_blocks = row_count // block_rows
    work_items = local_heads * row_blocks
    query_heads = query_rot.transpose(1, 0, 2)
    new_places = jnp.arange(NEW)[None, :]

    def block_place(index):
        head = index // row_blocks
        block = index % row_blocks
        owner = block // req_blocks
        query_pos = block % req_blocks * block_rows + jnp.arange(block_rows)
        query_part = lax.dynamic_slice(
            query_heads, (head, block * block_rows, 0), (1, block_rows, HD)
        )[0]
        return (head, owner, query_pos, query_part)

    incoming = lax.all_to_all(outgoing, "req", split_axis=0, concat_axis=0, tiled=True)
    spill_chunk = 8

    def spill_pages(chunk):
        wanted = chunk * spill_chunk + jnp.arange(spill_chunk)
        match = spill_flat[None, :] & (spill_pos[None, :] == wanted[:, None])
        owner = jnp.sum(jnp.where(match, holders_flat[None, :], 0), axis=1)
        slot = jnp.sum(jnp.where(match, slots_flat[None, :], 0), axis=1)
        mine = jnp.any(match, axis=1) & (owner == req_index)
        contrib = jnp.where(mine[:, None, None, None], kv_pool[slot], jnp.zeros((), kv_pool.dtype))
        return lax.psum(contrib, "req")

    own_holders = lax.dynamic_index_in_dim(holder_rows, req_index, 0, keepdims=False)
    own_rank = lax.dynamic_index_in_dim(rank_all, req_index, 0, keepdims=False)
    own_pos = lax.dynamic_index_in_dim(
        spill_pos.reshape(all_rows, -1), req_index, 0, keepdims=False
    )
    first_spill = spill_pages(0)
    source = jnp.concatenate([incoming, first_spill], axis=0)
    pick = jnp.where(own_rank == 0, own_holders, req_count + jnp.clip(own_pos, 0, spill_chunk - 1))
    fetched = source[pick]

    def more_cond(carry):
        chunk, _ = carry
        return chunk * spill_chunk < spill_count

    def more_body(carry):
        chunk, pages = carry
        got = spill_pages(chunk)
        local = own_pos - chunk * spill_chunk
        hit = (own_rank > 0) & (local >= 0) & (local < spill_chunk)
        pages = jnp.where(hit[:, None, None, None], got[jnp.clip(local, 0, spill_chunk - 1)], pages)
        return (chunk + 1, pages)

    _, fetched = lax.while_loop(more_cond, more_body, (jnp.int32(1), fetched))
    fetched = fetched.reshape(local_reqs, MAXP, 2, PAGE, local_width)
    cache_key = fetched[:, :, 0].reshape(local_reqs, cache_span, local_heads, HD)
    cache_value = fetched[:, :, 1].reshape(local_reqs, cache_span, local_heads, HD)
    keys_all = jnp.concatenate(
        [cache_key, new_key.reshape(local_reqs, NEW, local_heads, HD)], axis=1
    )
    values_all = jnp.concatenate(
        [cache_value, new_value.reshape(local_reqs, NEW, local_heads, HD)], axis=1
    )

    def joined_block(index):
        head, owner, query_pos, query_part = block_place(index)
        keys_part = lax.dynamic_slice(
            keys_all, (owner, 0, head, 0), (1, cache_span + NEW, 1, HD)
        ).reshape(cache_span + NEW, HD)
        values_part = lax.dynamic_slice(
            values_all, (owner, 0, head, 0), (1, cache_span + NEW, 1, HD)
        ).reshape(cache_span + NEW, HD)
        live_one = lax.dynamic_index_in_dim(live_len, owner, 0, keepdims=False)
        cache_ok = jnp.broadcast_to(
            jnp.arange(cache_span)[None, :] < live_one, (block_rows, cache_span)
        )
        allowed = jnp.concatenate([cache_ok, new_places <= query_pos[:, None]], axis=1)
        summed, row_top, row_total = attend_block(query_part, keys_part, values_part, allowed)
        return (summed / row_total[:, None]).astype(jnp.bfloat16)

    blocks_out = lax.map(joined_block, jnp.arange(work_items))
    attended = (
        blocks_out.reshape(local_heads, row_count, HD)
        .transpose(1, 0, 2)
        .reshape(row_count, local_width)
    )
    head_term = jnp.dot(attended, out_weight, preferred_element_type=jnp.float32)
    return lax.psum_scatter(head_term.astype(jnp.bfloat16), "tp", scatter_dimension=0, tiled=True)


def solution(mesh):
    in_specs = (
        P("req", None),
        P(None, None, "tp"),
        P("tp", None),
        P("req", None, None, "tp"),
        P(),
        P(),
        P(),
        P(),
    )
    out_specs = P(("req", "tp"), None)
    return jax.shard_map(body, mesh=mesh, in_specs=in_specs, out_specs=out_specs, check_vma=False)
```

profile of v0, /device:TPU:4, one launch (start us, length us, event | category | flops | bytes accessed | tf_op | source)
XLA Modules:
  0.0 353.3 jit_solution(13241626098705244110)
XLA Ops:
  6.5 1.7 convert_reduce_fusion.1
  8.2 1.4 convert_reduce_fusion.2
  9.6 4.3 %gather_fusion.2 = bf16[32,2,128,256]{3,2,1,0:T(8,128)(2,1)} fusion(bf16[16,2,128,256]{3,2,1,0:T(8,128)(2,1)} %param.15, s32[1024]{0:T(1024)S(1)} %pad_clamp_fusion.4), kind=kCustom, calls=%fused_computation.2 | custom fusion | bytes 8388736 | tf_op jit(solution)/shard_map/gather | solution.py:60
  13.9 11.8 %all-to-all-start = ((bf16[32,2,128,256]{3,2,1,0:T(8,128)(2,1)}), bf16[32,2,128,256]{3,2,1,0:T(8,128)(2,1)}, u32[]{:S(2)}, u32[]{:S(2)}) async-start(bf16[32,2,128,256]{3,2,1,0:T(8,128)(2,1)} %gather_fusion.2), calls=%async_computation | async-start | bytes 8388608 | tf_op jit(solution)/shard_map/all_to_all | solution.py:99
  26.9 0.7 reduce.10
  28.1 3.2 gather_fusion.3
  31.4 2.3 broadcast_select_fusion.2
  34.2 0.6 dynamic-slice.1
  35.4 0.6 dynamic_slice.46
  36.0 2.8 convert_reduce_fusion
  38.8 1.2 fusion.42
  40.1 4.0 %fusion.45 = f32[1024,3,256]{0,2,1:T(8,128)S(1)} fusion(bf16[2048,3,256]{2,0,1:T(8,128)(2,1)S(1)} %copy-done, bf16[1024,2048]{1,0:T(8,128)(2,1)S(1)} %copy-done.3, f32[1024]{0:T(1024)S(1)} %add_rsqrt_fusion, f32[1024]{0:T(1024)S(1)} %broadcast_multiply_fusion), kind=kOutput, calls=%fused_computation.53 | convolution fusion | flops 3229614080 | bytes 10493952 | tf_op jit(solution)/shard_map/td,dcf->tcf/dot_general | solution.py:74
  44.1 0.9 slice.84
  46.3 0.6 fusion.58
  46.9 0.6 fusion.59
  47.6 1.0 multiply_cosine_fusion
  48.8 1.1 fusion.49
  49.8 0.9 maximum_bitcast_fusion
  50.7 159.2 %all-reduce.3.cloned.1.call-done = bf16[8,2,128,256]{3,2,1,0:T(8,128)(2,1)} async-done(((bf16[8,2,128,256]{3,2,1,0:T(8,128)(2,1)}), bf16[8,2,128,256]{3,2,1,0:T(8,128)(2,1)}) %all-reduce.3.cloned.1.call-update) | async-done | bytes 1048592 | tf_op jit(solution)/shard_map/psum | solution.py:109
  210.0 5.3 %pad_maximum_fusion = bf16[40,2,128,256]{3,2,1,0:T(8,128)(2,1)} fusion(bf16[8,2,128,256]{3,2,1,0:T(8,128)(2,1)} %all-reduce.3.cloned.1.call-done, bf16[32,2,128,256]{3,2,1,0:T(8,128)(2,1)} %all-to-all-done), kind=kLoop, calls=%fused_computation.51 | loop fusion | flops 2621440 | bytes 10485760 | tf_op jit(solution)/shard_map/concatenate | solution.py:117
  215.2 5.5 %gather_fusion.4 = bf16[32,2,128,256]{3,2,1,0:T(8,128)(2,1)} fusion(bf16[40,2,128,256]{3,2,1,0:T(8,128)(2,1)} %pad_maximum_fusion, s32[1024]{0:T(1024)S(1)} %pad_clamp_fusion.2), kind=kCustom, calls=%fused_computation.4 | custom fusion | bytes 8388736 | tf_op jit(solution)/shard_map/gather | solution.py:119
  221.5 4.1 %fusion.62 = (bf16[1,32,1,128,256]{4,3,2,1,0:T(8,128)(2,1)}, bf16[1,32,1,128,256]{4,3,2,1,0:T(8,128)(2,1)S(1)}) fusion(bf16[1,32,2,128,256]{4,3,2,1,0:T(8,128)(2,1)} %bitcast.120), kind=kLoop, calls=%fused_computation.106 | loop fusion | bytes 8388608 | tf_op jit(solution)/shard_map/slice | solution.py:136
  225.6 2.0 reshape.422
  227.6 4.7 %copy.37 = bf16[1,4096,2,128]{1,3,2,0:T(8,128)(2,1)S(1)} copy(bf16[1,4096,2,128]{3,2,1,0:T(2,128)(2,1)} %reshape.422) | data formatting | bytes 4194304 | tf_op jit(solution)/shard_map/reshape;squeeze | solution.py:135
  232.4 4.1 %reshape.423 = bf16[1,4096,2,128]{3,2,1,0:T(2,128)(2,1)} reshape(bf16[1,32,1,128,256]{4,3,2,1,0:T(8,128)(2,1)} %get-tuple-element.250) | data formatting | bytes 4194304 | tf_op jit(solution)/shard_map/reshape;squeeze | solution.py:136
  236.4 6.2 %copy.38 = bf16[1,4096,2,128]{1,3,2,0:T(8,128)(2,1)} copy(bf16[1,4096,2,128]{3,2,1,0:T(2,128)(2,1)} %reshape.423) | data formatting | bytes 4194304 | tf_op jit(solution)/shard_map/reshape;squeeze | solution.py:136
  242.7 3.3 pad_maximum_fusion.1
  246.0 1.7 maximum_maximum_fusion
  247.7 52.4 %while.24 = (s32[]{:T(128)}, bf16[4,512,128]{2,1,0:T(8,128)(2,1)}, s32[1]{0:T(128)}, s32[4]{0:T(128)S(1)}, bf16[2,1024,128]{1,2,0:T(8,128)(2,1)}, /*index=5*/bf1...) while((s32[]{:T(128)}, bf16[4,512,128]{2,1,0:T(8,128)(2,1)}, ...), condition=%wide.region_20.21_spmd.clone, body=%wide.region_17.20_spmd.clone.sunk | while | flops 1374293504 | bytes 46969404 | solution.py:160
  247.7 0.6 dynamic_slice.107
  251.3 4.4 %fusion.80 = (f32[512]{0:T(512)S(1)}, f32[512,5120]{1,0:T(8,128)S(1)}) fusion(bf16[1,5120,2,128]{1,3,2,0:T(8,128)(2,1)} %get-tuple-element.523, s32[]{:T(128)S(6)} %select_n.234, bf16[2,1024,128]{1,2,0:T(8,128)(2,1)} %get-tuple-element.522, s32[]{:T(128)S(6)} %select_n.236, pred[512,1024]{1,0:T(32,128)(4,1)S(1)} %iota_compare_fusion.6, ...), kind=kOutput, calls=%fused_computation.105.clone.1 | convolution fusion | flops 681573888 | bytes 12460544 | tf_op jit(solution)/shard_map/while/body/eval_jaxpr/qd,kd->qk/dot_general | solution.py:31
  255.8 2.5 fusion.81
  258.3 2.5 fusion.82
  260.8 0.6 dynamic_slice.107
  264.4 4.4 %fusion.80 = (f32[512]{0:T(512)S(1)}, f32[512,5120]{1,0:T(8,128)S(1)}) fusion(bf16[1,5120,2,128]{1,3,2,0:T(8,128)(2,1)} %get-tuple-element.523, s32[]{:T(128)S(6)} %select_n.234, bf16[2,1024,128]{1,2,0:T(8,128)(2,1)} %get-tuple-element.522, s32[]{:T(128)S(6)} %select_n.236, pred[512,1024]{1,0:T(32,128)(4,1)S(1)} %iota_compare_fusion.6, ...), kind=kOutput, calls=%fused_computation.105.clone.1 | convolution fusion | flops 681573888 | bytes 12460544 | tf_op jit(solution)/shard_map/while/body/eval_jaxpr/qd,kd->qk/dot_general | solution.py:31
  268.9 2.5 fusion.81
  271.4 2.5 fusion.82
  273.9 0.6 dynamic_slice.107
  277.5 4.4 %fusion.80 = (f32[512]{0:T(512)S(1)}, f32[512,5120]{1,0:T(8,128)S(1)}) fusion(bf16[1,5120,2,128]{1,3,2,0:T(8,128)(2,1)} %get-tuple-element.523, s32[]{:T(128)S(6)} %select_n.234, bf16[2,1024,128]{1,2,0:T(8,128)(2,1)} %get-tuple-element.522, s32[]{:T(128)S(6)} %select_n.236, pred[512,1024]{1,0:T(32,128)(4,1)S(1)} %iota_compare_fusion.6, ...), kind=kOutput, calls=%fused_computation.105.clone.1 | convolution fusion | flops 681573888 | bytes 12460544 | tf_op jit(solution)/shard_map/while/body/eval_jaxpr/qd,kd->qk/dot_general | solution.py:31
  282.0 2.5 fusion.81
  284.5 2.5 fusion.82
  287.0 0.6 dynamic_slice.107
  290.6 4.4 %fusion.80 = (f32[512]{0:T(512)S(1)}, f32[512,5120]{1,0:T(8,128)S(1)}) fusion(bf16[1,5120,2,128]{1,3,2,0:T(8,128)(2,1)} %get-tuple-element.523, s32[]{:T(128)S(6)} %select_n.234, bf16[2,1024,128]{1,2,0:T(8,128)(2,1)} %get-tuple-element.522, s32[]{:T(128)S(6)} %select_n.236, pred[512,1024]{1,0:T(32,128)(4,1)S(1)} %iota_compare_fusion.6, ...), kind=kOutput, calls=%fused_computation.105.clone.1 | convolution fusion | flops 681573888 | bytes 12460544 | tf_op jit(solution)/shard_map/while/body/eval_jaxpr/qd,kd->qk/dot_general | solution.py:31
  295.1 2.5 fusion.81
  297.6 2.5 fusion.82
  300.1 2.0 copy.35
  302.1 4.8 %convolution_convert_fusion = bf16[1024,2048]{1,0:T(8,128)(2,1)} fusion(bf16[1024,256]{0,1:T(8,128)(2,1)} %bitcast.123, bf16[256,2048]{1,0:T(8,128)(2,1)} %param.14), kind=kOutput, calls=%fused_computation.56 | convolution fusion | flops 1075838976 | bytes 5767168 | tf_op jit(solution)/shard_map/dot_general | solution.py:166
  306.9 39.6 %reduce-scatter.2.cloned.1.call-done = bf16[128,2048]{1,0:T(8,128)(2,1)} async-done(((bf16[1024,2048]{1,0:T(8,128)(2,1)}), bf16[128,2048]{1,0:T(8,128)(2,1)}) %reduce-scatter.2.cloned.1.call-update) | async-done | bytes 524304 | tf_op jit(solution)/shard_map/reduce_scatter | solution.py:167
  (85 shorter events, 5.4 us)
Async XLA Ops:
  6.5 33.5 %copy-start = (bf16[2048,3,256]{2,0,1:T(8,128)(2,1)S(1)}, bf16[2048,3,256]{2,0,1:T(8,128)(2,1)}, u32[]{:S(2)}) copy-start(bf16[2048,3,256]{2,0,1:T(8,128)(2,1)} %param.13) | copy-start | bytes 9437188
  9.6 24.2 %copy-start.9 = (pred[32,32]{1,0:T(8,128)(4,1)}, pred[32,32]{1,0:T(8,128)(4,1)S(1)}, u32[]{:S(2)}) copy-start(pred[32,32]{1,0:T(8,128)(4,1)S(1)} %get-tuple-element.447) | copy-start | bytes 3076
  13.9 12.0 %copy-start.8 = (s32[32,32]{1,0:T(8,128)S(1)}, s32[32,32]{1,0:T(8,128)}, u32[]{:S(2)}) copy-start(s32[32,32]{1,0:T(8,128)} %param.17) | copy-start | bytes 12292
  13.9 13.0 %copy-start.6 = (s32[32,32,1]{1,2,0:T(1,128)S(1)}, s32[32,32,1]{1,2,0:T(1,128)}, u32[]{:S(2)}) copy-start(s32[32,32,1]{1,2,0:T(1,128)} %param.18) | copy-start | bytes 12292
  13.9 196.0 %all-to-all-start = ((bf16[32,2,128,256]{3,2,1,0:T(8,128)(2,1)}), bf16[32,2,128,256]{3,2,1,0:T(8,128)(2,1)}, u32[]{:S(2)}, u32[]{:S(2)}) async-start(bf16[32,2,128,256]{3,2,1,0:T(8,128)(2,1)} %gather_fusion.2), calls=%async_computation | async-start | bytes 8388608 | tf_op jit(solution)/shard_map/all_to_all | solution.py:99
  25.7 9.1 %copy-start.10 = (s32[32]{0:T(128)S(1)}, s32[32]{0:T(128)}, u32[]{:S(2)}) copy-start(s32[32]{0:T(128)} %param.16) | copy-start | bytes 388
  25.7 9.6 %copy-start.11 = (s32[32]{0:T(128)S(1)}, s32[32]{0:T(128)}, u32[]{:S(2)}) copy-start(s32[32]{0:T(128)} %param.19) | copy-start | bytes 388
  25.8 184.2 %all-reduce.3.cloned.1.call-start = ((), (), s32[]{:S(2)}) async-start(), calls=%async_computation.2 | async-start | bytes 2097152 | tf_op jit(solution)/shard_map/psum | solution.py:109
  34.2 4.7 %copy-start.3 = (bf16[1024,2048]{1,0:T(8,128)(2,1)S(1)}, bf16[1024,2048]{1,0:T(8,128)(2,1)}, u32[]{:S(2)}) copy-start(bf16[1024,2048]{1,0:T(8,128)(2,1)} %param.12) | copy-start | bytes 12582916
  215.2 5.5 %copy-start.2 = (bf16[16,2,128,256]{3,2,1,0:T(8,128)(2,1)S(1)}, bf16[16,2,128,256]{3,2,1,0:T(8,128)(2,1)}, u32[]{:S(2)}) copy-start(bf16[16,2,128,256]{3,2,1,0:T(8,128)(2,1)} %param.15) | copy-start | bytes 6291460
  221.3 125.2 %reduce-scatter.2.cloned.1.call-start = ((), (), s32[]{:S(2)}) async-start(), calls=%async_computation.3 | async-start | bytes 4718592 | tf_op jit(solution)/shard_map/reduce_scatter | solution.py:167
  232.4 10.3 %copy-start.5 = (bf16[1024,1,256]{0,2,1:T(8,128)(2,1)S(1)}, bf16[1024,1,256]{0,2,1:T(8,128)(2,1)}, u32[]{:S(2)}) copy-start(bf16[1024,1,256]{0,2,1:T(8,128)(2,1)} %slice.84) | copy-start | bytes 1572868
  236.4 9.5 %copy-start.7 = (bf16[1,1024,2,64]{1,3,2,0:T(8,128)(2,1)S(1)}, bf16[1,1024,2,64]{1,3,2,0:T(8,128)(2,1)}, u32[]{:S(2)}) copy-start(bf16[1,1024,2,64]{1,3,2,0:T(8,128)(2,1)} %get-tuple-element.255) | copy-start | bytes 786436
  255.8 2.5 copy-start.4
  268.9 2.5 copy-start.4
  282.0 2.5 copy-start.4
  295.1 2.5 copy-start.4
  302.1 44.3 %copy-start.1 = (bf16[2048,3,256]{2,0,1:T(8,128)(2,1)S(1)}, bf16[2048,3,256]{2,0,1:T(8,128)(2,1)}, u32[]{:S(2)}) copy-start(bf16[2048,3,256]{2,0,1:T(8,128)(2,1)} %param.13) | copy-start | bytes 9437188
Sparse Core Ops, SparseCore 0:
  33.9 176.0 all-reduce.2
  307.0 39.3 reduce-scatter.1
where the time goes:
time: 354 us; the launch traced here: 353 us
  waiting for transfers between devices  199 us (56%)
  local copies, waits for them, and re-layouts  43 us (12%)
  other arithmetic  36.8 us (10%)
  matrix products  36.5 us (10%)
  between operations  14.8 us (4%)
  starting transfers between devices  12 us (3%)
  loops' own time  11.3 us (3%)
    psum x1, waiting for transfers between devices, spill_pages(): return lax.psum(contrib, 'req')  159 us
    reduce_scatter x1, waiting for transfers between devices, body(): lax.psum_scatter(head_term.astype(jnp.bfloat16), 'tp', scatter_dimension=...  39.6 us
    dot_general x4, matrix products, attend_block(): jnp.einsum('qd,kd->qk', query_part, keys_part, preferred_element_type=jnp...  17.7 us
    all_to_all x1, starting transfers between devices, body(): lax.all_to_all(outgoing, 'req', split_axis=0, concat_axis=0, tiled=True)  11.8 us
    another operation x1, loops' own time, body(): blocks_out = lax.map(joined_block, jnp.arange(work_items))  10.7 us
    another operation x2, local copies, waits for them, and re-layouts, body(): fetched[:, :, 1].reshape(local_reqs, cache_span, local_heads, HD)  10.3 us
    dot_general x4, matrix products, attend_block(): jnp.einsum('qk,kd->qd', weights.astype(jnp.bfloat16), values_part, prefer...  9.99 us
    reduce_sum x4, other arithmetic, attend_block(): row_total = jnp.sum(weights, axis=-1)  9.99 us
  transfers between devices with their start and end apart: 3, of which 2 were waited for; matrix products, arithmetic and copies ran while one was open for 7% of the time, Pallas kernels for 0%

commit v1 on v0

--- a/solution.py
+++ b/solution.py
@@ -106,7 +106,7 @@
         slot = jnp.sum(jnp.where(match, slots_flat[None, :], 0), axis=1)
         mine = jnp.any(match, axis=1) & (owner == req_index)
         contrib = jnp.where(mine[:, None, None, None], kv_pool[slot], jnp.zeros((), kv_pool.dtype))
-        return lax.psum(contrib, "req")
+        return jnp.sum(lax.all_gather(contrib, "req"), axis=0)
 
     own_holders = lax.dynamic_index_in_dim(holder_rows, req_index, 0, keepdims=False)
     own_rank = lax.dynamic_index_in_dim(rank_all, req_index, 0, keepdims=False)

time: 354 us -> 492 us (1.39)
  waiting for transfers between devices: 199 us -> 326 us
  other arithmetic: 36.8 us -> 47.5 us
    all_gather x0 -> x1, waiting for transfers between devices: none -> 287 us  [spill_pages(): return jnp.sum(lax.all_gather(contrib, 'req'), axis=0)]
    psum x1 -> x0, waiting for transfers between devices: 159 us -> none  [spill_pages(): return lax.psum(contrib, 'req')]
    reduce_sum x0 -> x1, other arithmetic: none -> 11.4 us  [spill_pages(): return jnp.sum(lax.all_gather(contrib, 'req'), axis=0)]
  transfers between devices with their start and end apart: 3 -> 3, of which waited for: 2 -> 2; matrix products, arithmetic and copies ran while one was open for 7% -> 6% of each run, Pallas kernels for 0% -> 0%
where the time goes in v1:
time: 492 us; the launch traced here: 491 us
  waiting for transfers between devices  326 us (66%)
  other arithmetic  47.5 us (10%)
  local copies, waits for them, and re-layouts  43.8 us (9%)
  matrix products  36.5 us (7%)
  between operations  15 us (3%)
  starting transfers between devices  11.8 us (2%)
  loops' own time  10.4 us (2%)
    all_gather x1, waiting for transfers between devices, spill_pages(): return jnp.sum(lax.all_gather(contrib, 'req'), axis=0)  287 us
    reduce_scatter x1, waiting for transfers between devices, body(): lax.psum_scatter(head_term.astype(jnp.bfloat16), 'tp', scatter_dimension=...  39.2 us
    dot_general x4, matrix products, attend_block(): jnp.einsum('qd,kd->qk', query_part, keys_part, preferred_element_type=jnp...  17.8 us
    all_to_all x1, starting transfers between devices, body(): lax.all_to_all(outgoing, 'req', split_axis=0, concat_axis=0, tiled=True)  11.8 us
    reduce_sum x1, other arithmetic, spill_pages(): return jnp.sum(lax.all_gather(contrib, 'req'), axis=0)  11.4 us
    another operation x2, local copies, waits for them, and re-layouts, body(): fetched[:, :, 1].reshape(local_reqs, cache_span, local_heads, HD)  10.3 us
    reduce_sum x4, other arithmetic, attend_block(): row_total = jnp.sum(weights, axis=-1)  9.99 us
    dot_general x4, matrix products, attend_block(): jnp.einsum('qk,kd->qd', weights.astype(jnp.bfloat16), values_part, prefer...  9.98 us
  transfers between devices with their start and end apart: 3, of which 2 were waited for; matrix products, arithmetic and copies ran while one was open for 6% of the time, Pallas kernels for 0%

profile of v1, /device:TPU:4, one launch (start us, length us, event | category | flops | bytes accessed | tf_op | source)
XLA Modules:
  0.0 491.1 jit_solution(2574243898929547694)
XLA Ops:
  6.6 1.7 convert_reduce_fusion.1
  8.2 1.5 convert_reduce_fusion.2
  9.8 0.8 broadcast_in_dim.160
  11.7 1.4 reduce.15
  13.5 3.2 gather_fusion.3
  16.7 2.3 bitcast_select_fusion.1
  19.1 4.4 gather_fusion.2
  23.5 11.8 %all-to-all-start = ((bf16[32,2,128,256]{3,2,1,0:T(8,128)(2,1)}), bf16[32,2,128,256]{3,2,1,0:T(8,128)(2,1)}, u32[]{:S(2)}, u32[]{:S(2)}) async-start(bf16[32,2,128,256]{3,2,1,0:T(8,128)(2,1)} %gather_fusion.2), calls=%async_computation | async-start | bytes 8388608 | tf_op jit(solution)/shard_map/all_to_all | solution.py:99
  35.6 0.7 dynamic-slice.1
  36.3 0.6 dynamic_slice.45
  36.9 0.6 dynamic_slice.46
  37.6 2.8 convert_reduce_fusion
  40.4 1.2 fusion.42
  41.6 4.0 fusion.45
  45.7 0.9 slice.84
  47.9 0.7 fusion.58
  48.6 0.6 fusion.60
  49.3 1.0 multiply_cosine_fusion
  50.5 1.1 fusion.49
  51.6 0.8 maximum_bitcast_fusion
  52.4 286.9 %all-gather.3.cloned.1.call-done = bf16[32,8,2,128,256]{4,3,2,1,0:T(8,128)(2,1)} async-done(((bf16[1,8,2,128,256]{4,3,2,1,0:T(8,128)(2,1)}), bf16[32,8,2,128,256]{4,3,2,1,0:T(8,128)(2,1)}) %all-gather.3.cloned.1.call-update) | async-done | bytes 33554448 | tf_op jit(solution)/shard_map/all_gather | solution.py:109
  339.3 11.4 %reduce_sum.137 = bf16[8,2,128,256]{3,2,1,0:T(8,128)(2,1)S(1)} reduce(bf16[32,8,2,128,256]{4,3,2,1,0:T(8,128)(2,1)} %all-gather.3.cloned.1.call-done, bf16[]{:T(256)} %constant.186.clone.1), dimensions={0}, to_apply=%region_9.10 | reduce | flops 16252928 | bytes 34603008 | tf_op jit(solution)/shard_map/reduce_sum | solution.py:109
  350.7 5.0 %pad_maximum_fusion = bf16[40,2,128,256]{3,2,1,0:T(8,128)(2,1)} fusion(bf16[8,2,128,256]{3,2,1,0:T(8,128)(2,1)S(1)} %reduce_sum.137, bf16[32,2,128,256]{3,2,1,0:T(8,128)(2,1)} %all-to-all-done), kind=kLoop, calls=%fused_computation.51 | loop fusion | flops 2621440 | bytes 10485760 | tf_op jit(solution)/shard_map/concatenate | solution.py:117
  355.7 5.5 %gather_fusion.4 = bf16[32,2,128,256]{3,2,1,0:T(8,128)(2,1)} fusion(bf16[40,2,128,256]{3,2,1,0:T(8,128)(2,1)} %pad_maximum_fusion, s32[1024]{0:T(1024)S(1)} %pad_clamp_fusion.2), kind=kCustom, calls=%fused_computation.4 | custom fusion | bytes 8388736 | tf_op jit(solution)/shard_map/gather | solution.py:119
  361.2 0.9 while.27
  362.1 4.1 fusion.62
  366.2 2.0 reshape.449
  368.2 4.7 copy.44
  373.0 4.1 reshape.450
  377.0 6.3 %copy.45 = bf16[1,4096,2,128]{1,3,2,0:T(8,128)(2,1)} copy(bf16[1,4096,2,128]{3,2,1,0:T(2,128)(2,1)} %reshape.450) | data formatting | bytes 4194304 | tf_op jit(solution)/shard_map/reshape;squeeze | solution.py:136
  383.3 3.8 maximum_maximum_fusion
  387.1 51.1 %while.26 = (s32[]{:T(128)}, bf16[4,512,128]{2,1,0:T(8,128)(2,1)}, s32[1]{0:T(128)}, s32[4]{0:T(128)S(1)}, bf16[2,1024,128]{1,2,0:T(8,128)(2,1)}, /*index=5*/bf1...) while((s32[]{:T(128)}, bf16[4,512,128]{2,1,0:T(8,128)(2,1)}, ...), condition=%wide.region_20.21_spmd.clone, body=%wide.region_17.20_spmd.clone.sunk | while | flops 1374293504 | bytes 46969404 | solution.py:160
  387.1 0.6 dynamic_slice.107
  390.4 4.4 fusion.80
  394.9 2.5 fusion.81
  397.4 2.5 fusion.82
  403.2 4.4 fusion.80
  407.7 2.5 fusion.81
  410.2 2.5 fusion.82
  416.0 4.4 fusion.80
  420.5 2.5 fusion.81
  423.0 2.5 fusion.82
  428.8 4.4 fusion.80
  433.2 2.5 fusion.81
  435.7 2.5 fusion.82
  438.2 2.0 copy.42
  440.3 4.8 convolution_convert_fusion
  445.1 39.2 %reduce-scatter.2.cloned.1.call-done = bf16[128,2048]{1,0:T(8,128)(2,1)} async-done(((bf16[1024,2048]{1,0:T(8,128)(2,1)}), bf16[128,2048]{1,0:T(8,128)(2,1)}) %reduce-scatter.2.cloned.1.call-update) | async-done | bytes 524304 | tf_op jit(solution)/shard_map/reduce_scatter | solution.py:167
  (86 shorter events, 5.7 us)
Async XLA Ops:
  6.5 35.1 %copy-start = (bf16[2048,3,256]{2,0,1:T(8,128)(2,1)S(1)}, bf16[2048,3,256]{2,0,1:T(8,128)(2,1)}, u32[]{:S(2)}) copy-start(bf16[2048,3,256]{2,0,1:T(8,128)(2,1)} %param.13) | copy-start | bytes 9437188
  6.5 332.8 %all-gather.3.cloned.1.call-start = ((), (), s32[]{:S(2)}) async-start(), calls=%async_computation.2 | async-start | bytes 34603008 | tf_op jit(solution)/shard_map/all_gather | solution.py:109
  9.7 25.6 %copy-start.9 = (pred[32,32]{1,0:T(8,128)(4,1)}, pred[32,32]{1,0:T(8,128)(4,1)S(1)}, u32[]{:S(2)}) copy-start(pred[32,32]{1,0:T(8,128)(4,1)S(1)} %get-tuple-element.536) | copy-start | bytes 3076
  23.5 11.9 %copy-start.8 = (s32[32,32]{1,0:T(8,128)S(1)}, s32[32,32]{1,0:T(8,128)}, u32[]{:S(2)}) copy-start(s32[32,32]{1,0:T(8,128)} %param.17) | copy-start | bytes 12292
  23.5 12.8 %copy-start.10 = (s32[32]{0:T(128)S(1)}, s32[32]{0:T(128)}, u32[]{:S(2)}) copy-start(s32[32]{0:T(128)} %param.16) | copy-start | bytes 388
  23.5 13.5 %copy-start.11 = (s32[32]{0:T(128)S(1)}, s32[32]{0:T(128)}, u32[]{:S(2)}) copy-start(s32[32]{0:T(128)} %param.19) | copy-start | bytes 388
  23.5 327.3 %all-to-all-start = ((bf16[32,2,128,256]{3,2,1,0:T(8,128)(2,1)}), bf16[32,2,128,256]{3,2,1,0:T(8,128)(2,1)}, u32[]{:S(2)}, u32[]{:S(2)}) async-start(bf16[32,2,128,256]{3,2,1,0:T(8,128)(2,1)} %gather_fusion.2), calls=%async_computation | async-start | bytes 8388608 | tf_op jit(solution)/shard_map/all_to_all | solution.py:99
  35.6 4.7 copy-start.3
  41.6 6.3 %copy-start.6 = (s32[32,32,1]{1,2,0:T(1,128)S(1)}, s32[32,32,1]{1,2,0:T(1,128)}, u32[]{:S(2)}) copy-start(s32[32,32,1]{1,2,0:T(1,128)} %param.18) | copy-start | bytes 12292
  355.7 5.5 %copy-start.2 = (bf16[16,2,128,256]{3,2,1,0:T(8,128)(2,1)S(1)}, bf16[16,2,128,256]{3,2,1,0:T(8,128)(2,1)}, u32[]{:S(2)}) copy-start(bf16[16,2,128,256]{3,2,1,0:T(8,128)(2,1)} %param.15) | copy-start | bytes 6291460
  362.1 122.2 %reduce-scatter.2.cloned.1.call-start = ((), (), s32[]{:S(2)}) async-start(), calls=%async_computation.3 | async-start | bytes 4718592 | tf_op jit(solution)/shard_map/reduce_scatter | solution.py:167
  373.0 10.3 %copy-start.5 = (bf16[1024,1,256]{0,2,1:T(8,128)(2,1)S(1)}, bf16[1024,1,256]{0,2,1:T(8,128)(2,1)}, u32[]{:S(2)}) copy-start(bf16[1024,1,256]{0,2,1:T(8,128)(2,1)} %slice.84) | copy-start | bytes 1572868
  373.0 10.3 %copy-start.7 = (bf16[1,1024,2,64]{1,3,2,0:T(8,128)(2,1)S(1)}, bf16[1,1024,2,64]{1,3,2,0:T(8,128)(2,1)}, u32[]{:S(2)}) copy-start(bf16[1,1024,2,64]{1,3,2,0:T(8,128)(2,1)} %get-tuple-element.344) | copy-start | bytes 786436
  394.9 2.5 copy-start.4
  407.7 2.5 copy-start.4
  420.4 2.5 copy-start.4
  433.2 2.5 copy-start.4
  440.3 44.0 %copy-start.1 = (bf16[2048,3,256]{2,0,1:T(8,128)(2,1)S(1)}, bf16[2048,3,256]{2,0,1:T(8,128)(2,1)}, u32[]{:S(2)}) copy-start(bf16[2048,3,256]{2,0,1:T(8,128)(2,1)} %param.13) | copy-start | bytes 9437188
Sparse Core Ops, SparseCore 0:
  19.2 320.0 all-gather.2
  445.2 39.0 reduce-scatter.1
